TPU v7x, 32 devices: a whole 2x2x4 slice. The times are simulated.
32 devices in a mesh: rows: 8 (over z, x), heads: 4 (over y, core).
Axes of the slice: x: 2, y: 2, z: 4, core: 2. Of those that a mesh axis runs over, the one named last changes fastest.
Arguments:
- patches: float32 [16384, 48], P(('rows', 'heads')), may hold values from -6 to 6
- segments: int32 [16384], P('rows'), may hold values from 0 to 3, as said below
- labels: int32 [64, 4], P(('rows', 'heads')), may hold values from 0 to 999
- w_in: bfloat16 [48, 768], replicated, may hold values from -0.875 to 0.875
- b_in: float32 [768], replicated, may hold values from -3 to 3
- pos_table: bfloat16 [256, 768], replicated, may hold values from -3 to 3
- cls_table: bfloat16 [1000, 768], replicated, may hold values from -3 to 3
- ln1_gain: float32 [1, 768], replicated, may hold values from 0.1 to 1.9
- ln1_bias: float32 [1, 768], replicated, may hold values from -2 to 2
- w_query: bfloat16 [1, 768, 768], P(None, None, 'heads'), may hold values from -0.21875 to 0.21875
- w_key: bfloat16 [1, 768, 768], P(None, None, 'heads'), may hold values from -0.21875 to 0.21875
- w_value: bfloat16 [1, 768, 768], P(None, None, 'heads'), may hold values from -0.21875 to 0.21875
- w_attn_out: bfloat16 [1, 768, 768], P(None, 'heads'), may hold values from -1.25 to 1.25
- ln2_gain: float32 [1, 768], replicated, may hold values from 0.1 to 1.9
- ln2_bias: float32 [1, 768], replicated, may hold values from -2 to 2
- w_up: bfloat16 [1, 768, 3072], P(None, None, 'heads'), may hold values from -0.21875 to 0.21875
- b_up: bfloat16 [1, 3072], P(None, 'heads'), may hold values from -3 to 3
- w_down: bfloat16 [1, 3072, 768], P(None, 'heads'), may hold values from -0.109375 to 0.109375
- b_down: float32 [1, 768], replicated, may hold values from -3 to 3
- w_out: bfloat16 [768, 96], replicated, may hold values from -0.02734375 to 0.02734375
- b_out: float32 [96], replicated, may hold values from -2 to 2
- latent_grad: float32 [16384, 48], P(('rows', 'heads')), may hold values from -6 to 6
- logdet_grad: float32 [16384], P(('rows', 'heads')), may hold values from -6 to 6
Outputs:
- latents: float32 [16384, 48], P(('rows', 'heads'))
- logdet: float32 [16384], P(('rows', 'heads'))
- patches_grad: float32 [16384, 48], P(('rows', 'heads'))
- scale_mean: float32 [64], P(('rows', 'heads'))
- scale_max: float32 [64], P(('rows', 'heads'))
- w_in_grad: float32 [48, 768], replicated
- b_in_grad: float32 [768], replicated
- pos_table_grad: float32 [256, 768], replicated
- cls_table_grad: float32 [1000, 768], replicated
- ln1_gain_grad: float32 [1, 768], replicated
- ln1_bias_grad: float32 [1, 768], replicated
- w_query_grad: float32 [1, 768, 768], P(None, None, 'heads')
- w_key_grad: float32 [1, 768, 768], P(None, None, 'heads')
- w_value_grad: float32 [1, 768, 768], P(None, None, 'heads')
- w_attn_out_grad: float32 [1, 768, 768], P(None, 'heads')
- ln2_gain_grad: float32 [1, 768], replicated
- ln2_bias_grad: float32 [1, 768], replicated
- w_up_grad: float32 [1, 768, 3072], P(None, None, 'heads')
- b_up_grad: float32 [1, 3072], P(None, 'heads')
- w_down_grad: float32 [1, 3072, 768], P(None, 'heads')
- b_down_grad: float32 [1, 768], replicated
- w_out_grad: float32 [768, 96], replicated
- b_out_grad: float32 [96], replicated
Inputs may be any that keep to these rules, and one draw needn't show every extreme that they name: Each row of 256 patches is either one segment numbered 0, or 4 segments of 64 patches numbered 0 to 3 in order; the first row is of the second kind.
All inputs are finite; a program needn't handle non-finite values.
Results may differ from a plain program's by a relative error of at most 0.034.
Values may be sent and summed in bfloat16 or wider, within the bound.
No kernel may reach another device: no remote copies, remote signals or barrier semaphores. Data moves between devices by JAX's collectives and lax.ppermute only.
A program may use at most 128 MiB of HBM per device.

v0:
```python
import jax
import jax.numpy as jnp
from jax import lax
from jax.sharding import PartitionSpec as P

HEAD_DIM = 64
EPSILON = 1e-05
PRECISE = lax.Precision.HIGHEST


def norm_rows(values, gains, offset):
    average = jnp.mean(values, -1, keepdims=True)
    centered = values - average
    spread = jnp.mean(centered * centered, -1, keepdims=True)
    return centered * lax.rsqrt(spread + EPSILON) * gains + offset


def gelu_exact(values):
    return jax.nn.gelu(values, approximate=False)


def matmul(matrix, other):
    return jnp.dot(matrix, other, preferred_element_type=jnp.float32)


def matmul_tn(matrix, other):
    return lax.dot_general(
        matrix, other, (((0,), (0,)), ((), ())), preferred_element_type=jnp.float32
    )


def matmul_nt(matrix, other):
    return lax.dot_general(
        matrix, other, (((1,), (1,)), ((), ())), preferred_element_type=jnp.float32
    )


def masked_scores(queries, key_rows, seg_block):
    length = seg_block.shape[-1]
    causal = lax.broadcasted_iota(jnp.int32, (length, length), 0) >= lax.broadcasted_iota(
        jnp.int32, (length, length), 1
    )
    allowed = (seg_block[:, :, None] == seg_block[:, None, :]) & causal[None]
    scores = jnp.einsum("bqhe,bkhe->bhqk", queries, key_rows, preferred_element_type=jnp.float32)
    return jnp.where(allowed[:, None], scores * HEAD_DIM ** (-0.5), -1e30)


def attend_forward(pieces):
    queries, key_rows, values, seg_block = pieces
    scores = masked_scores(queries, key_rows, seg_block)
    row_top = jnp.max(scores, -1, keepdims=True)
    denominator = jnp.sum(jnp.exp(scores - row_top), -1, keepdims=True)
    log_total = row_top + jnp.log(denominator)
    probs = jnp.exp(scores - log_total).astype(jnp.bfloat16)
    result = jnp.einsum("bhqk,bkhe->bqhe", probs, values, preferred_element_type=jnp.float32)
    return (result.astype(jnp.bfloat16), log_total)


def attend_backward(pieces):
    queries, key_rows, values, seg_block, log_total, grad_result = pieces
    scores = masked_scores(queries, key_rows, seg_block)
    probs = jnp.exp(scores - log_total)
    grad_probs = jnp.einsum(
        "bqhe,bkhe->bhqk", grad_result, values, preferred_element_type=jnp.float32
    )
    inner_sum = jnp.sum(probs * grad_probs, -1, keepdims=True)
    grad_scores = (probs * (grad_probs - inner_sum) * HEAD_DIM ** (-0.5)).astype(jnp.bfloat16)
    grad_query = jnp.einsum(
        "bhqk,bkhe->bqhe", grad_scores, key_rows, preferred_element_type=jnp.float32
    )
    grad_key = jnp.einsum(
        "bhqk,bqhe->bkhe", grad_scores, queries, preferred_element_type=jnp.float32
    )
    grad_value = jnp.einsum(
        "bhqk,bqhe->bkhe",
        probs.astype(jnp.bfloat16),
        grad_result,
        preferred_element_type=jnp.float32,
    )
    return (
        grad_query.astype(jnp.bfloat16),
        grad_key.astype(jnp.bfloat16),
        grad_value.astype(jnp.bfloat16),
    )


def per_device(
    patches,
    segments,
    labels,
    w_in,
    b_in,
    pos_table,
    cls_table,
    ln1_gain,
    ln1_bias,
    w_query,
    w_key,
    w_value,
    w_attn_out,
    ln2_gain,
    ln2_bias,
    w_up,
    b_up,
    w_down,
    b_down,
    w_out,
    b_out,
    latent_grad,
    logdet_grad,
):
    tokens_here = patches.shape[0]
    length = pos_table.shape[0]
    slot_count = labels.shape[1]
    channels = patches.shape[1]
    classes = cls_table.shape[0]
    width = pos_table.shape[1]
    heads_here = w_query.shape[2] // HEAD_DIM
    layers = w_query.shape[0]
    own_start = lax.axis_index("heads") * tokens_here
    own_segs = lax.dynamic_slice_in_dim(segments, own_start, tokens_here)
    seg_rows = own_segs.reshape(-1, length)
    row_count = seg_rows.shape[0]
    causal = lax.broadcasted_iota(jnp.int32, (length, length), 0) >= lax.broadcasted_iota(
        jnp.int32, (length, length), 1
    )
    matching = (seg_rows[:, :, None] == seg_rows[:, None, :]) & causal[None]
    position = (jnp.sum(matching.astype(jnp.int32), -1) - 1).reshape(-1)
    slot_ids = lax.broadcasted_iota(jnp.int32, (1, 1, slot_count), 2)
    token_label = jnp.sum(
        jnp.where(seg_rows[:, :, None] == slot_ids, labels[:, None, :], 0), -1
    ).reshape(-1)
    pos_onehot = (position[:, None] == lax.broadcasted_iota(jnp.int32, (1, length), 1)).astype(
        jnp.bfloat16
    )
    cls_onehot = (token_label[:, None] == lax.broadcasted_iota(jnp.int32, (1, classes), 1)).astype(
        jnp.bfloat16
    )
    patch_low = patches.astype(jnp.bfloat16)
    hidden = (
        matmul(patch_low, w_in)
        + b_in
        + matmul(pos_onehot, pos_table)
        + matmul(cls_onehot, cls_table)
    )
    group_rows = segments.shape[0] // length
    blocks = group_rows // 2
    seg_blocks = segments.reshape(blocks, 2, length)

    def to_blocks(matrix):
        return matrix.reshape(blocks, 2, length, heads_here, HEAD_DIM)

    def from_blocks(tensor):
        return tensor.reshape(group_rows * length, heads_here * HEAD_DIM)

    depth = 0
    normed1 = norm_rows(hidden, ln1_gain[depth], ln1_bias[depth]).astype(jnp.bfloat16)
    rows_norm = lax.all_gather(normed1, "heads", axis=0, tiled=True)
    queries = matmul(rows_norm, w_query[depth]).astype(jnp.bfloat16)
    key_rows = matmul(rows_norm, w_key[depth]).astype(jnp.bfloat16)
    values = matmul(rows_norm, w_value[depth]).astype(jnp.bfloat16)
    attended, log_total = lax.map(
        attend_forward, (to_blocks(queries), to_blocks(key_rows), to_blocks(values), seg_blocks)
    )
    attended = from_blocks(attended)
    weight_out = w_attn_out[depth]
    attn_mix = lax.psum_scatter(
        matmul(attended, weight_out).astype(jnp.bfloat16), "heads", scatter_dimension=0, tiled=True
    ).astype(jnp.float32)
    hidden1 = hidden + attn_mix
    normed2 = norm_rows(hidden1, ln2_gain[depth], ln2_bias[depth]).astype(jnp.bfloat16)
    mlp_input = lax.all_gather(normed2, "heads", axis=0, tiled=True)
    full_up = w_up[depth]
    full_bias = b_up[depth]
    full_down = w_down[depth]
    pre_act = matmul(mlp_input, full_up) + full_bias.astype(jnp.float32)
    activated = gelu_exact(pre_act).astype(jnp.bfloat16)
    branch = lax.psum_scatter(
        matmul(activated, full_down).astype(jnp.bfloat16), "heads", scatter_dimension=0, tiled=True
    ).astype(jnp.float32)
    hidden2 = hidden1 + branch + b_down[depth]
    stored = [
        (
            hidden,
            rows_norm,
            queries,
            key_rows,
            values,
            attended,
            log_total,
            hidden1,
            mlp_input,
            pre_act,
            activated,
            full_up,
            full_down,
        )
    ]
    top_low = hidden2.astype(jnp.bfloat16)
    head_out = matmul(top_low, w_out) + b_out
    carried = jnp.concatenate(
        [jnp.zeros((row_count, 1), dtype=bool), seg_rows[:, 1:] == seg_rows[:, :-1]], 1
    ).reshape(-1)

    def flow_head(head_vals, patch_vals):
        previous = jnp.concatenate([jnp.zeros_like(head_vals[:1]), head_vals[:-1]], 0)
        previous = jnp.where(carried[:, None], previous, 0.0)
        shifts = previous[:, :channels]
        logscale = previous[:, channels:]
        latent_vals = (patch_vals - shifts) * jnp.exp(-logscale)
        return ((latent_vals, -jnp.sum(logscale, -1)), logscale)

    (latents, logdet), head_pull, logscale = jax.vjp(flow_head, head_out, patches, has_aux=True)
    grad_head, grad_direct = head_pull((latent_grad, logdet_grad))
    scale_rows = logscale.reshape(row_count, -1)
    scale_mean = jnp.mean(scale_rows, -1)
    scale_max = jnp.max(scale_rows, -1)
    grad_low = grad_head.astype(jnp.bfloat16)
    grad_w_out = matmul_tn(top_low, grad_low)
    grad_b_out = jnp.sum(grad_low.astype(jnp.float32), 0)
    grad_hidden = matmul_nt(grad_low, w_out)
    per_layer = [None] * layers
    for depth in reversed(range(layers)):
        (
            hidden0,
            rows_norm,
            queries,
            key_rows,
            values,
            attended,
            log_total,
            hidden1,
            mlp_input,
            pre_act,
            activated,
            full_up,
            full_down,
        ) = stored[depth]
        grad_b_down = jnp.sum(grad_hidden, 0)
        grad_branch = grad_hidden.astype(jnp.bfloat16)
        grad_branch_rows = lax.all_gather(grad_branch, "heads", axis=0, tiled=True)
        grad_activated = matmul_nt(grad_branch_rows, full_down)
        gelu_values, gelu_pull = jax.vjp(gelu_exact, pre_act)
        grad_pre = gelu_pull(grad_activated)[0].astype(jnp.bfloat16)
        grad_w_down = matmul_tn(activated, grad_branch_rows)
        grad_w_up = matmul_tn(mlp_input, grad_pre)
        grad_b_up = jnp.sum(grad_pre.astype(jnp.float32), 0)
        grad_normed2 = lax.psum_scatter(
            matmul_nt(grad_pre, full_up).astype(jnp.bfloat16),
            "heads",
            scatter_dimension=0,
            tiled=True,
        ).astype(jnp.float32)
        norm_values, norm_pull = jax.vjp(norm_rows, hidden1, ln2_gain[depth], ln2_bias[depth])
        back_hidden1, grad_gain2, grad_bias2 = norm_pull(grad_normed2)
        grad_hidden1 = grad_hidden + back_hidden1
        grad_mix = grad_hidden1.astype(jnp.bfloat16)
        grad_mix_rows = lax.all_gather(grad_mix, "heads", axis=0, tiled=True)
        weight_out = w_attn_out[depth]
        grad_attended = matmul_nt(grad_mix_rows, weight_out).astype(jnp.bfloat16)
        grad_w_attn = matmul_tn(attended, grad_mix_rows)
        grad_query, grad_key, grad_value = lax.map(
            attend_backward,
            (
                to_blocks(queries),
                to_blocks(key_rows),
                to_blocks(values),
                seg_blocks,
                log_total,
                to_blocks(grad_attended),
            ),
        )
        grad_query = from_blocks(grad_query)
        grad_key = from_blocks(grad_key)
        grad_value = from_blocks(grad_value)
        grad_w_query = matmul_tn(rows_norm, grad_query)
        grad_w_key = matmul_tn(rows_norm, grad_key)
        grad_w_value = matmul_tn(rows_norm, grad_value)
        weight_query, weight_key, weight_value = (w_query[depth], w_key[depth], w_value[depth])
        total = matmul_nt(grad_query, weight_query)
        total = total + matmul_nt(grad_key, weight_key)
        grad_normed1 = lax.psum_scatter(
            (total + matmul_nt(grad_value, weight_value)).astype(jnp.bfloat16),
            "heads",
            scatter_dimension=0,
            tiled=True,
        ).astype(jnp.float32)
        norm_values1, norm_pull1 = jax.vjp(norm_rows, hidden0, ln1_gain[depth], ln1_bias[depth])
        back_hidden0, grad_gain1, grad_bias1 = norm_pull1(grad_normed1)
        grad_hidden = grad_hidden1 + back_hidden0
        per_layer[depth] = (
            grad_w_query,
            grad_w_key,
            grad_w_value,
            grad_w_attn,
            grad_w_up,
            grad_b_up,
            grad_w_down,
            grad_gain1,
            grad_bias1,
            grad_gain2,
            grad_bias2,
            grad_b_down,
        )

    def stacked(index):
        return jnp.stack([entry[index] for entry in per_layer], 0)

    grad_embed = grad_hidden.astype(jnp.bfloat16)
    grad_w_in = matmul_tn(patch_low, grad_embed)
    grad_b_in = jnp.sum(grad_embed.astype(jnp.float32), 0)
    patches_grad = grad_direct + matmul_nt(grad_embed, w_in)
    quarter = length // slot_count
    packed_row = seg_rows[:, -1] > 0
    grad_slots = grad_hidden.reshape(row_count, slot_count, quarter, width)
    single_part = jnp.sum(
        jnp.where(packed_row[:, None, None], 0.0, grad_hidden.reshape(row_count, length, width)), 0
    )
    packed_part = jnp.sum(jnp.where(packed_row[:, None, None, None], grad_slots, 0.0), (0, 1))
    grad_pos = single_part + jnp.concatenate(
        [packed_part, jnp.zeros((length - quarter, width), jnp.float32)], 0
    )
    slot_sums = jnp.sum(grad_slots, 2)
    row_total = jnp.sum(slot_sums, 1)
    first_slot = lax.broadcasted_iota(jnp.int32, (1, slot_count, 1), 1) == 0
    slot_vectors = jnp.where(
        packed_row[:, None, None], slot_sums, jnp.where(first_slot, row_total[:, None, :], 0.0)
    )
    label_onehot = (
        labels.reshape(-1)[:, None] == lax.broadcasted_iota(jnp.int32, (1, classes), 1)
    ).astype(jnp.float32)
    grad_cls = lax.dot_general(
        label_onehot, slot_vectors.reshape(-1, width), (((0,), (0,)), ((), ())), precision=PRECISE
    )
    sum_query, sum_key, sum_value, sum_attn, sum_up, sum_b_up, sum_down = lax.psum(
        (stacked(0), stacked(1), stacked(2), stacked(3), stacked(4), stacked(5), stacked(6)), "rows"
    )
    (
        sum_w_in,
        sum_b_in,
        sum_pos,
        sum_cls,
        sum_gain1,
        sum_bias1,
        sum_gain2,
        sum_bias2,
        sum_b_down,
        sum_w_out,
        sum_b_out,
    ) = lax.psum(
        (
            grad_w_in,
            grad_b_in,
            grad_pos,
            grad_cls,
            stacked(7),
            stacked(8),
            stacked(9),
            stacked(10),
            stacked(11),
            grad_w_out,
            grad_b_out,
        ),
        ("rows", "heads"),
    )
    return (
        latents,
        logdet,
        patches_grad,
        scale_mean,
        scale_max,
        sum_w_in,
        sum_b_in,
        sum_pos,
        sum_cls,
        sum_gain1,
        sum_bias1,
        sum_query,
        sum_key,
        sum_value,
        sum_attn,
        sum_gain2,
        sum_bias2,
        sum_up,
        sum_b_up,
        sum_down,
        sum_b_down,
        sum_w_out,
        sum_b_out,
    )


def solution(mesh):
    in_specs = (
        P(("rows", "heads"), None),
        P("rows"),
        P(("rows", "heads"), None),
        P(),
        P(),
        P(),
        P(),
        P(),
        P(),
        P(None, None, "heads"),
        P(None, None, "heads"),
        P(None, None, "heads"),
        P(None, "heads", None),
        P(),
        P(),
        P(None, None, "heads"),
        P(None, "heads"),
        P(None, "heads", None),
        P(),
        P(),
        P(),
        P(("rows", "heads"), None),
        P(("rows", "heads")),
    )
    out_specs = (
        P(("rows", "heads"), None),
        P(("rows", "heads")),
        P(("rows", "heads"), None),
        P(("rows", "heads")),
        P(("rows", "heads")),
        P(),
        P(),
        P(),
        P(),
        P(),
        P(),
        P(None, None, "heads"),
        P(None, None, "heads"),
        P(None, None, "heads"),
        P(None, "heads", None),
        P(),
        P(),
        P(None, None, "heads"),
        P(None, "heads"),
        P(None, "heads", None),
        P(),
        P(),
        P(),
    )
    return jax.shard_map(
        per_device, mesh=mesh, in_specs=in_specs, out_specs=out_specs, check_vma=False
    )
```

profile of v0, /device:TPU:0, one launch (start us, length us, event | category | flops | bytes accessed | tf_op | source)
XLA Modules:
  0.0 903.8 jit_solution(2534567188782438305)
XLA Ops:
  14.6 31.1 %all-gather.5.cloned.1.call-done = bf16[2048,768]{1,0:T(8,128)(2,1)} async-done(((bf16[512,768]{1,0:T(8,128)(2,1)}), bf16[2048,768]{1,0:T(8,128)(2,1)}) %all-gather.5.cloned.1.call-update) | async-done | bytes 3145744 | tf_op jit(solution)/shard_map/all_gather | solution.py:158
  45.7 3.1 convolution_convert_fusion.8
  51.6 3.9 convolution_convert_fusion.7
  55.5 3.3 reshape.257
  58.8 2.2 copy.80
  61.0 3.9 convolution_convert_fusion.6
  64.9 3.2 reshape.258
  68.2 2.2 copy.81
  71.7 12.9 %while.26 = (s32[]{:T(128)}, bf16[4,2,256,3,64]{2,1,0,4,3:T(2,128)(2,1)}, f32[4,2,3,256,1]{3,2,1,4,0:T(4,128)S(1)}, bf16[4,2,256,3,64]{2,4,3,1,0:T(8,128)(2,1)S(...) while((s32[]{:T(128)}, ...), condition=%wide.region_7.8_spmd, body=%wide.region_4.7_spmd.sunk | while | flops 103840256 | bytes 6358625 | solution.py:162
  85.5 2.5 reshape.259
  88.0 2.7 convolution_convert_fusion.4
  91.4 37.4 %reduce-scatter.5.cloned.1.call-done = bf16[512,768]{1,0:T(8,128)(2,1)} async-done(((bf16[2048,768]{1,0:T(8,128)(2,1)}), bf16[512,768]{1,0:T(8,128)(2,1)}) %reduce-scatter.5.cloned.1.call-update) | async-done | bytes 786448 | tf_op jit(solution)/shard_map/reduce_scatter | solution.py:167
  132.9 28.4 %all-gather.7.cloned.1.call-done = bf16[2048,768]{1,0:T(8,128)(2,1)} async-done(((bf16[512,768]{1,0:T(8,128)(2,1)}), bf16[2048,768]{1,0:T(8,128)(2,1)}) %all-gather.7.cloned.1.call-update) | async-done | bytes 3145744 | tf_op jit(solution)/shard_map/all_gather | solution.py:172
  161.3 18.8 %multiply_convert_fusion.1 = (bf16[2048,768]{1,0:T(8,128)(2,1)S(1)}, f32[2048,768]{1,0:T(8,128)}, f32[2048,768]{1,0:T(8,128)}) fusion(f32[768]{0:T(1024)S(1)} %convert_reduce_fusion.6, bf16[2048,768]{1,0:T(8,128)(2,1)} %all-gather.7.cloned.1.call-done, bf16[1,768,768]{2,1,0:T(8,128)(2,1)} %param.42), kind=kOutput, calls=%fused_computation.70 | convolution fusion | flops 2519728128 | bytes 20057088 | tf_op jit(solution)/shard_map/dot_general | solution.py:23
  181.8 3.9 convolution_convert_fusion.3
  186.7 37.1 %reduce-scatter.7.cloned.1.call-done = bf16[512,768]{1,0:T(8,128)(2,1)} async-done(((bf16[2048,768]{1,0:T(8,128)(2,1)}), bf16[512,768]{1,0:T(8,128)(2,1)}) %reduce-scatter.7.cloned.1.call-update) | async-done | bytes 786448 | tf_op jit(solution)/shard_map/reduce_scatter | solution.py:178
  223.8 1.8 add_convert_fusion.2
  228.0 1.8 fusion.125
  229.8 28.6 %all-gather.9.cloned.1.call-done = bf16[2048,768]{1,0:T(8,128)(2,1)} async-done(((bf16[512,768]{1,0:T(8,128)(2,1)}), bf16[2048,768]{1,0:T(8,128)(2,1)}) %all-gather.9.cloned.1.call-update) | async-done | bytes 3145744 | tf_op jit(solution)/shard_map/all_gather | solution.py:241
  258.5 11.2 %convert_reduce_fusion = (f32[768]{0:T(1024)}, bf16[2048,768]{1,0:T(8,128)(2,1)S(1)}) fusion(f32[2048,768]{1,0:T(8,128)} %get-tuple-element.240, bf16[2048,768]{1,0:T(8,128)(2,1)} %all-gather.9.cloned.1.call-done, bf16[1,768,768]{2,1,0:T(8,128)(2,1)} %param.44, f32[2048,768]{1,0:T(8,128)} %get-tuple-element.255, f32[768]{0:T(1024)S(1)} %convert_reduce_fusion.6), kind=kOutput, calls=%fused_computation.67 | convolution fusion | flops 2442657024 | bytes 20060160 | tf_op jit(solution)/shard_map/dot_general | solution.py:33
  271.3 4.0 convolution_convert_fusion.2
  275.8 37.7 %reduce-scatter.9.cloned.1.call-done = bf16[512,768]{1,0:T(8,128)(2,1)} async-done(((bf16[2048,768]{1,0:T(8,128)(2,1)}), bf16[512,768]{1,0:T(8,128)(2,1)}) %reduce-scatter.9.cloned.1.call-update) | async-done | bytes 786448 | tf_op jit(solution)/shard_map/reduce_scatter | solution.py:248
  313.5 3.0 fusion.69
  316.5 2.2 fusion.120
  321.0 28.6 %all-gather.11.cloned.1.call-done = bf16[2048,768]{1,0:T(8,128)(2,1)} async-done(((bf16[512,768]{1,0:T(8,128)(2,1)}), bf16[2048,768]{1,0:T(8,128)(2,1)}) %all-gather.11.cloned.1.call-update) | async-done | bytes 3145744 | tf_op jit(solution)/shard_map/all_gather | solution.py:258
  349.7 3.9 convolution_convert_fusion.5
  353.6 3.3 reshape.260
  360.8 69.2 %while.27 = (s32[]{:T(128)}, bf16[4,2,256,3,64]{2,1,0,4,3:T(2,128)(2,1)}, bf16[4,2,256,3,64]{2,1,0,4,3:T(2,128)(2,1)}, bf16[4,2,256,3,64]{2,1,0,4,3:T(2,128)(2,1...) while((s32[]{:T(128)}, ...), condition=%wide.region_18.19_spmd, body=%wide.region_16.18_spmd.sunk | while | flops 257789440 | bytes 21261944 | solution.py:262
  361.0 2.7 subtract_exponential_fusion.2
  364.8 2.5 fusion.187
  367.3 3.5 fusion.190
  373.8 3.5 fusion.188
  378.3 2.7 subtract_exponential_fusion.2
  382.1 2.5 fusion.187
  384.6 3.5 fusion.190
  388.1 1.8 fusion.189
  391.1 3.5 fusion.188
  395.6 2.7 subtract_exponential_fusion.2
  399.4 2.5 fusion.187
  401.9 3.5 fusion.190
  405.4 1.8 fusion.189
  408.4 3.4 fusion.188
  412.9 2.7 subtract_exponential_fusion.2
  416.7 2.5 fusion.187
  419.2 3.5 fusion.190
  422.7 1.8 fusion.189
  425.7 3.4 fusion.188
  430.0 3.1 reshape.263
  433.1 3.2 reshape.262
  436.3 3.3 reshape.261
  439.7 2.3 fusion.83
  443.1 2.8 add_convert_fusion
  446.1 7.1 convolution_bitcast_fusion
  453.1 4.1 convolution_bitcast_fusion.1
  466.6 17.5 %reduce-scatter.11.cloned.1.call-done = bf16[512,768]{1,0:T(8,128)(2,1)} async-done(((bf16[2048,768]{1,0:T(8,128)(2,1)}), bf16[512,768]{1,0:T(8,128)(2,1)}) %reduce-scatter.11.cloned.1.call-update) | async-done | bytes 786448 | tf_op jit(solution)/shard_map/reduce_scatter | solution.py:282
  484.1 1.8 convert_reduce_fusion.1
  489.5 1.8 select_reduce_fusion.1
  493.4 3.3 fusion.101
  498.8 22.7 %psum.139 = f32[1,768]{1,0:T(1,128)} all-reduce(f32[1,768]{1,0:T(1,128)S(1)} %stack.33), channel_id=1, replica_groups=mesh['rows'=8,'heads'=4] {'rows'}, use_global_device_ids=true, to_apply=%region_48.49 | all-reduce | flops 768 | bytes 6144 | tf_op jit(solution)/shard_map/psum | solution.py:335
  521.5 41.5 %all-reduce.6 = (f32[768]{0:T(1024)}, f32[1,768]{1,0:T(1,128)}, f32[1,768]{1,0:T(1,128)}, f32[1,768]{1,0:T(1,128)}, f32[1,768]{1,0:T(1,128)}, /*index=5*/f32[1,768]{1,0:T(1,128)}, f32[96]{0:T(128)}) all-reduce(f32[768]{0:T(1024)S(1)} %get-tuple-element.235, ...), channel_id=1, replica_groups=mesh['rows'=8,'heads'=4] {'rows','heads'}, use_global_device_ids=true, to_apply=%region_27.28 | all-reduce | flops 4704 | bytes 37632 | tf_op jit(solution)/shard_map/psum | solution.py:350
  564.0 165.1 %all-reduce.14.cloned.1.call-done = (f32[1,768,192]{1,2,0:T(8,128)}, f32[1,768,192]{1,2,0:T(8,128)}, f32[1,768,192]{1,2,0:T(8,128)}, f32[1,192,768]{2,1,0:T(8,12...) async-done(((f32[1,768,192]{1,2,0:T(8,128)}, f32[1,768,192]{1,2,0:T(8,128)}, f32[1,768,192]{1,2,0:T(8,128)}, f32[1,192,768]{2,1,0:T(8,128)}, f32[1,768,768]{2,1,0:T(8,128)}, ...) | async-done | bytes 7077904 | tf_op jit(solution)/shard_map/psum | solution.py:335
  729.1 152.3 %all-reduce.12.cloned.1.call-done = (f32[48,768]{1,0:T(8,128)}, f32[256,768]{1,0:T(8,128)}, f32[1000,768]{1,0:T(8,128)}, f32[768,96]{0,1:T(8,128)}) async-done(((f32[48,768]{1,0:T(8,128)}, f32[256,768]{1,0:T(8,128)}, f32[1000,768]{1,0:T(8,128)}, f32[768,96]{0,1:T(8,128)}), (f32[48,768]{1,0:T(8,128)}, f32[256,768]{1,0:T(8,128)}, f32[1000,768]{1,0:T(8,128)}, ...) | async-done | bytes 4300816 | tf_op jit(solution)/shard_map/psum | solution.py:350
  882.9 2.1 copy.162
  885.0 3.8 copy.163
  (300 shorter events, 86.9 us)
Async XLA Ops:
  7.2 3.9 copy-start
  7.2 3.5 copy-start.23
  7.2 3.5 copy-start.36
  7.2 38.5 %all-gather.5.cloned.1.call-start = ((), (), s32[]{:S(2)}) async-start(), calls=%async_computation.4 | async-start | bytes 3932160 | tf_op jit(solution)/shard_map/all_gather | solution.py:158
  9.2 1.8 copy-start.59
  13.1 1.5 copy-start.44
  13.1 32.6 %copy-start.40 = (bf16[1,768,192]{1,2,0:T(8,128)(2,1)S(1)}, bf16[1,768,192]{1,2,0:T(8,128)(2,1)}, u32[]{:S(2)}) copy-start(bf16[1,768,192]{1,2,0:T(8,128)(2,1)} %param.38) | copy-start | bytes 884740
  14.3 114.5 %reduce-scatter.5.cloned.1.call-start = ((), (), s32[]{:S(2)}) async-start(), calls=%async_computation.5 | async-start | bytes 3932160 | tf_op jit(solution)/shard_map/reduce_scatter | solution.py:167
  48.8 2.8 copy-start.33
  55.5 5.5 copy-start.31
  85.5 2.5 copy-start.38
  90.7 70.6 %all-gather.7.cloned.1.call-start = ((), (), s32[]{:S(2)}) async-start(), calls=%async_computation.6 | async-start | bytes 3932160 | tf_op jit(solution)/shard_map/all_gather | solution.py:172
  130.2 1.1 copy-start.2
  131.3 1.5 copy-start.47
  132.6 91.2 %reduce-scatter.7.cloned.1.call-start = ((), (), s32[]{:S(2)}) async-start(), calls=%async_computation.7 | async-start | bytes 3932160 | tf_op jit(solution)/shard_map/reduce_scatter | solution.py:178
  161.3 20.5 %copy-start.57 = (bf16[1,768,768]{2,1,0:T(8,128)(2,1)S(1)}, bf16[1,768,768]{2,1,0:T(8,128)(2,1)}, u32[]{:S(2)}) copy-start(bf16[1,768,768]{2,1,0:T(8,128)(2,1)} %param.44) | copy-start | bytes 3538948
  180.1 1.7 copy-start.60
  185.7 72.8 %all-gather.9.cloned.1.call-start = ((), (), s32[]{:S(2)}) async-start(), calls=%async_computation.8 | async-start | bytes 3932160 | tf_op jit(solution)/shard_map/all_gather | solution.py:241
  186.7 38.9 %copy-start.24 = (bf16[768,96]{0,1:T(8,128)(2,1)S(1)}, bf16[768,96]{0,1:T(8,128)(2,1)}, u32[]{:S(2)}) copy-start(bf16[768,96]{0,1:T(8,128)(2,1)} %param.46) | copy-start | bytes 442372
  186.7 39.3 %copy-start.55 = (f32[96]{0:T(128)S(1)}, f32[96]{0:T(128)}, u32[]{:S(2)}) copy-start(f32[96]{0:T(128)} %param.47) | copy-start | bytes 1156
  225.6 4.2 copy-start.16
  225.6 1.0 copy-start.29
  229.8 83.7 %reduce-scatter.9.cloned.1.call-start = ((), (), s32[]{:S(2)}) async-start(), calls=%async_computation.9 | async-start | bytes 3932160 | tf_op jit(solution)/shard_map/reduce_scatter | solution.py:248
  258.5 12.8 %copy-start.58 = (bf16[1,768,768]{2,1,0:T(8,128)(2,1)S(1)}, bf16[1,768,768]{2,1,0:T(8,128)(2,1)}, u32[]{:S(2)}) copy-start(bf16[1,768,768]{2,1,0:T(8,128)(2,1)} %param.42) | copy-start | bytes 3538948
  269.6 1.7 copy-start.61
  275.4 74.3 %all-gather.11.cloned.1.call-start = ((), (), s32[]{:S(2)}) async-start(), calls=%async_computation.10 | async-start | bytes 3932160 | tf_op jit(solution)/shard_map/all_gather | solution.py:258
  313.5 3.0 copy-start.20
  316.5 3.4 copy-start.6
  318.6 1.2 copy-start.8
  319.9 29.8 %copy-start.39 = (bf16[1,192,768]{2,1,0:T(8,128)(2,1)S(1)}, bf16[1,192,768]{2,1,0:T(8,128)(2,1)}, u32[]{:S(2)}) copy-start(bf16[1,192,768]{2,1,0:T(8,128)(2,1)} %param.39) | copy-start | bytes 884740
  321.0 163.1 %reduce-scatter.11.cloned.1.call-start = ((), (), s32[]{:S(2)}) async-start(), calls=%async_computation.11 | async-start | bytes 3932160 | tf_op jit(solution)/shard_map/reduce_scatter | solution.py:282
  433.1 6.5 copy-start.32
  439.6 2.3 copy-start.12
  439.6 2.3 copy-start.34
  441.9 1.1 copy-start.14
  441.9 1.2 copy-start.41
  446.0 283.1 %all-reduce.14.cloned.1.call-start = ((), (), s32[]{:S(2)}) async-start(), calls=%async_computation.13 | async-start | bytes 14155776 | tf_op jit(solution)/shard_map/psum | solution.py:335
  446.0 7.1 copy-start.56
  446.0 7.1 copy-start.62
  453.1 4.1 copy-start.19
  457.3 2.1 copy-start.5
  457.3 2.3 copy-start.15
  459.6 1.6 copy-start.11
  461.2 1.6 copy-start.13
  464.4 1.2 copy-start.17
  464.5 416.9 %all-reduce.12.cloned.1.call-start = ((), (), s32[]{:S(2)}) async-start(), calls=%async_computation.12 | async-start | bytes 8601600 | tf_op jit(solution)/shard_map/psum | solution.py:350
  484.1 1.9 copy-start.18
  484.1 2.8 copy-start.9
  485.9 1.4 copy-start.7
  488.1 1.1 copy-start.3
  489.4 1.9 copy-start.4
  496.7 2.1 copy-start.46
  496.7 24.8 %copy-start.43 = (f32[768]{0:T(1024)S(1)}, f32[768]{0:T(1024)}, u32[]{:S(2)}) copy-start(f32[768]{0:T(1024)} %get-tuple-element.173) | copy-start | bytes 9220
  496.7 24.8 %copy-start.42 = (f32[768]{0:T(1024)S(1)}, f32[768]{0:T(1024)}, u32[]{:S(2)}) copy-start(f32[768]{0:T(1024)} %get-tuple-element.177) | copy-start | bytes 9220
  496.7 66.3 %copy-start.30 = (f32[512,48]{0,1:T(8,128)S(1)}, f32[512,48]{0,1:T(8,128)}, u32[]{:S(2)}) copy-start(f32[512,48]{0,1:T(8,128)} %param.48) | copy-start | bytes 294916
  496.7 66.3 %copy-start.37 = (bf16[48,768]{1,0:T(8,128)(2,1)S(1)}, bf16[48,768]{1,0:T(8,128)(2,1)}, u32[]{:S(2)}) copy-start(bf16[48,768]{1,0:T(8,128)(2,1)} %param.30) | copy-start | bytes 221188
  885.0 3.8 copy-start.28
  885.0 4.6 copy-start.27
  888.8 1.6 copy-start.26
  888.8 2.5 copy-start.25
  889.6 2.5 copy-start.22
  892.1 2.5 copy-start.21
  892.1 4.6 copy-start.1
  894.6 1.4 copy-start.35
  (9 other events, 6.6 us)
Sparse Core Ops, SparseCore 0:
  14.5 31.2 all-gather.4
  90.8 37.9 reduce-scatter.4
  132.7 28.5 all-gather.6
  185.8 37.9 reduce-scatter.6
  229.9 28.5 all-gather.8
  275.5 37.9 reduce-scatter.8
  321.1 28.5 all-gather.10
  446.1 37.9 reduce-scatter.10
  490.3 238.7 all-reduce.13
  737.9 143.3 all-reduce.11
where the time goes:
time: 908 us; the launch traced here: 904 us
  waiting for transfers between devices  564 us (62%)
  matrix products  154 us (17%)
  local copies, waits for them, and re-layouts  78.6 us (9%)
  blocking collectives  64.2 us (7%)
  other arithmetic  26.4 us (3%)
  between operations  15.1 us (2%)
    psum x1, waiting for transfers between devices, per_device(): lax.psum((stacked(0), stacked(1), stacked(2), stacked(3), stacked(4), sta...  165 us
    psum x1, waiting for transfers between devices, per_device(): lax.psum((grad_w_in, grad_b_in, grad_pos, grad_cls, stacked(7), stacked(8...  152 us
    psum x1, blocking collectives, per_device(): lax.psum((grad_w_in, grad_b_in, grad_pos, grad_cls, stacked(7), stacked(8...  41.5 us
    dot_general x10, matrix products, matmul(): return jnp.dot(matrix, other, preferred_element_type=jnp.float32)  39.8 us
    reduce_scatter x1, waiting for transfers between devices, per_device(): lax.psum_scatter(matmul_nt(grad_pre, full_up).astype(jnp.bfloat16), 'head...  37.7 us
    reduce_scatter x1, waiting for transfers between devices, per_device(): lax.psum_scatter(matmul(attended, weight_out).astype(jnp.bfloat16), 'head...  37.4 us
    reduce_scatter x1, waiting for transfers between devices, per_device(): lax.psum_scatter(matmul(activated, full_down).astype(jnp.bfloat16), 'head...  37.1 us
    all_gather x1, waiting for transfers between devices, per_device(): rows_norm = lax.all_gather(normed1, 'heads', axis=0, tiled=True)  31.1 us
  transfers between devices with their start and end apart: 10, of which 10 were waited for; matrix products, arithmetic and copies ran while one was open for 4% of the time, Pallas kernels for 0%

commit v1 on v0

--- a/solution.py
+++ b/solution.py
@@ -238,7 +238,40 @@
         ) = stored[depth]
         grad_b_down = jnp.sum(grad_hidden, 0)
         grad_branch = grad_hidden.astype(jnp.bfloat16)
-        grad_branch_rows = lax.all_gather(grad_branch, "heads", axis=0, tiled=True)
+        newest = jax.lax.axis_index("heads")
+        z = jax.lax.axis_size("heads")
+        current_block, b_now, block_out = (z, newest, grad_branch.shape[0])
+        nodes = []
+        ix = 0
+        while ix < current_block:
+            nodes.append((ix, (ix + 1) % current_block))
+            ix += 1
+        buffers = []
+        ix = 0
+        while ix < current_block:
+            buffers.append((ix, (ix - 1) % current_block))
+            ix = ix + 1
+        grad_branch_rows = jnp.zeros(
+            (*grad_branch.shape[:0], current_block * block_out, *grad_branch.shape[0 + 1 :]),
+            grad_branch.dtype,
+        )
+        y = f_now = grad_branch
+        grad_branch_rows = lax.dynamic_update_slice_in_dim(
+            grad_branch_rows, grad_branch, b_now * block_out, axis=0
+        )
+        c = 1
+        passed = current_block // 2
+        while c < passed + 1:
+            y = jax.lax.ppermute(y, axis_name="heads", perm=nodes)
+            grad_branch_rows = lax.dynamic_update_slice_in_dim(
+                grad_branch_rows, y, (b_now - c) % current_block * block_out, axis=0
+            )
+            if c < current_block - passed:
+                f_now = jax.lax.ppermute(f_now, axis_name="heads", perm=buffers)
+                grad_branch_rows = lax.dynamic_update_slice_in_dim(
+                    grad_branch_rows, f_now, (b_now + c) % current_block * block_out, axis=0
+                )
+            c += 1
         grad_activated = matmul_nt(grad_branch_rows, full_down)
         gelu_values, gelu_pull = jax.vjp(gelu_exact, pre_act)
         grad_pre = gelu_pull(grad_activated)[0].astype(jnp.bfloat16)

time: 908 us -> 914 us (level)
    all_gather x1 -> x0, waiting for transfers between devices: 28.6 us -> none  [per_device(): grad_branch_rows = lax.all_gather(grad_branch, 'heads', axis=0, tiled=True)]
    ppermute x0 -> x3, waiting for transfers between devices: none -> 25.3 us  [the longest x2 25.3 us: per_device(): y = jax.lax.ppermute(y, axis_name='heads', perm=nodes)]
  transfers between devices with their start and end apart: 10 -> 12, of which waited for: 10 -> 11; matrix products, arithmetic and copies ran while one was open for 4% -> 4% of each run, Pallas kernels for 0% -> 0%
where the time goes in v1:
time: 914 us; the launch traced here: 910 us
  waiting for transfers between devices  560 us (61%)
  matrix products  154 us (17%)
  local copies, waits for them, and re-layouts  86.4 us (9%)
  blocking collectives  64.3 us (7%)
  other arithmetic  27.5 us (3%)
  between operations  14.8 us (2%)
    psum x1, waiting for transfers between devices, per_device(): lax.psum((stacked(0), stacked(1), stacked(2), stacked(3), stacked(4), sta...  164 us
    psum x1, waiting for transfers between devices, per_device(): lax.psum((grad_w_in, grad_b_in, grad_pos, grad_cls, stacked(7), stacked(8...  152 us
    psum x1, blocking collectives, per_device(): lax.psum((grad_w_in, grad_b_in, grad_pos, grad_cls, stacked(7), stacked(8...  41.2 us
    dot_general x10, matrix products, matmul(): return jnp.dot(matrix, other, preferred_element_type=jnp.float32)  40.7 us
    reduce_scatter x1, waiting for transfers between devices, per_device(): lax.psum_scatter(matmul_nt(grad_pre, full_up).astype(jnp.bfloat16), 'head...  37.8 us
    reduce_scatter x1, waiting for transfers between devices, per_device(): lax.psum_scatter(matmul(attended, weight_out).astype(jnp.bfloat16), 'head...  37.4 us
    reduce_scatter x1, waiting for transfers between devices, per_device(): lax.psum_scatter(matmul(activated, full_down).astype(jnp.bfloat16), 'head...  37.2 us
    all_gather x1, waiting for transfers between devices, per_device(): rows_norm = lax.all_gather(normed1, 'heads', axis=0, tiled=True)  31.1 us
  transfers between devices with their start and end apart: 12, of which 11 were waited for; matrix products, arithmetic and copies ran while one was open for 4% of the time, Pallas kernels for 0%

profile of v1, /device:TPU:0, one launch (start us, length us, event | category | flops | bytes accessed | tf_op | source)
XLA Modules:
  0.0 910.0 jit_solution(6197123498587982954)
XLA Ops:
  15.1 31.1 %all-gather.4.cloned.1.call-done = bf16[2048,768]{1,0:T(8,128)(2,1)} async-done(((bf16[512,768]{1,0:T(8,128)(2,1)}), bf16[2048,768]{1,0:T(8,128)(2,1)}) %all-gather.4.cloned.1.call-update) | async-done | bytes 3145744 | tf_op jit(solution)/shard_map/all_gather | solution.py:158
  46.3 3.1 convolution_convert_fusion.8
  52.1 3.9 convolution_convert_fusion.7
  56.1 3.3 reshape.257
  59.4 2.2 copy.80
  61.6 3.9 convolution_convert_fusion.6
  65.5 3.2 reshape.258
  68.7 2.2 copy.81
  72.2 12.9 %while.26 = (s32[]{:T(128)}, bf16[4,2,256,3,64]{2,1,0,4,3:T(2,128)(2,1)}, f32[4,2,3,256,1]{3,2,1,4,0:T(4,128)S(1)}, bf16[4,2,256,3,64]{2,4,3,1,0:T(8,128)(2,1)S(...) while((s32[]{:T(128)}, ...), condition=%wide.region_7.8_spmd, body=%wide.region_4.7_spmd.sunk | while | flops 103840256 | bytes 6358625 | solution.py:162
  86.0 2.4 reshape.259
  88.5 2.7 convolution_convert_fusion.4
  91.9 37.4 %reduce-scatter.5.cloned.1.call-done = bf16[512,768]{1,0:T(8,128)(2,1)} async-done(((bf16[2048,768]{1,0:T(8,128)(2,1)}), bf16[512,768]{1,0:T(8,128)(2,1)}) %reduce-scatter.5.cloned.1.call-update) | async-done | bytes 786448 | tf_op jit(solution)/shard_map/reduce_scatter | solution.py:167
  133.3 28.4 %all-gather.6.cloned.1.call-done = bf16[2048,768]{1,0:T(8,128)(2,1)} async-done(((bf16[512,768]{1,0:T(8,128)(2,1)}), bf16[2048,768]{1,0:T(8,128)(2,1)}) %all-gather.6.cloned.1.call-update) | async-done | bytes 3145744 | tf_op jit(solution)/shard_map/all_gather | solution.py:172
  161.7 18.8 %multiply_convert_fusion.1 = (bf16[2048,768]{1,0:T(8,128)(2,1)S(1)}, f32[2048,768]{1,0:T(8,128)}, f32[2048,768]{1,0:T(8,128)}) fusion(f32[768]{0:T(1024)S(1)} %convert_reduce_fusion.6, bf16[2048,768]{1,0:T(8,128)(2,1)} %all-gather.6.cloned.1.call-done, bf16[1,768,768]{2,1,0:T(8,128)(2,1)} %param.42), kind=kOutput, calls=%fused_computation.70 | convolution fusion | flops 2519728128 | bytes 20057088 | tf_op jit(solution)/shard_map/dot_general | solution.py:23
  182.3 3.9 convolution_convert_fusion.3
  187.2 37.2 %reduce-scatter.7.cloned.1.call-done = bf16[512,768]{1,0:T(8,128)(2,1)} async-done(((bf16[2048,768]{1,0:T(8,128)(2,1)}), bf16[512,768]{1,0:T(8,128)(2,1)}) %reduce-scatter.7.cloned.1.call-update) | async-done | bytes 786448 | tf_op jit(solution)/shard_map/reduce_scatter | solution.py:178
  229.0 1.9 broadcast_in_dim.183
  230.9 2.1 constant_dynamic-update-slice_fusion.3
  234.7 17.9 %collective-permute-done = bf16[512,768]{1,0:T(8,128)(2,1)} collective-permute-done((bf16[512,768]{1,0:T(8,128)(2,1)}, bf16[512,768]{1,0:T(8,128)(2,1)}, u32[]{:S(2)}, u32[]{:S(2)}) %collective-permute-start) | collective-permute-done | bytes 786464 | tf_op jit(solution)/shard_map/ppermute | solution.py:265
  252.5 2.2 constant_dynamic-update-slice_fusion.2
  254.7 2.1 constant_dynamic-update-slice_fusion.1
  256.8 7.5 collective-permute-done.2
  264.3 2.1 constant_dynamic-update-slice_fusion
  266.3 10.1 %convert_reduce_fusion = (f32[768]{0:T(1024)}, bf16[2048,768]{1,0:T(8,128)(2,1)S(1)}) fusion(f32[2048,768]{1,0:T(8,128)} %get-tuple-element.242, bf16[2048,768]{1,0:T(8,128)(2,1)} %constant_dynamic-update-slice_fusion, bf16[1,768,768]{2,1,0:T(8,128)(2,1)S(1)} %copy-done.57, f32[2048,768]{1,0:T(8,128)} %get-tuple-element.257, f32[768]{0:T(1024)S(1)} %convert_reduce_fusion.6), kind=kOutput, calls=%fused_computation.67 | convolution fusion | flops 2442657024 | bytes 20060160 | tf_op jit(solution)/shard_map/dot_general | solution.py:33
  278.2 4.0 convolution_convert_fusion.2
  282.3 37.8 %reduce-scatter.9.cloned.1.call-done = bf16[512,768]{1,0:T(8,128)(2,1)} async-done(((bf16[2048,768]{1,0:T(8,128)(2,1)}), bf16[512,768]{1,0:T(8,128)(2,1)}) %reduce-scatter.9.cloned.1.call-update) | async-done | bytes 786448 | tf_op jit(solution)/shard_map/reduce_scatter | solution.py:281
  320.1 3.0 fusion.69
  323.1 2.2 fusion.120
  328.0 28.2 %all-gather.8.cloned.1.call-done = bf16[2048,768]{1,0:T(8,128)(2,1)} async-done(((bf16[512,768]{1,0:T(8,128)(2,1)}), bf16[2048,768]{1,0:T(8,128)(2,1)}) %all-gather.8.cloned.1.call-update) | async-done | bytes 3145744 | tf_op jit(solution)/shard_map/all_gather | solution.py:291
  356.3 3.9 convolution_convert_fusion.5
  360.2 3.3 reshape.260
  367.4 69.2 %while.27 = (s32[]{:T(128)}, bf16[4,2,256,3,64]{2,1,0,4,3:T(2,128)(2,1)}, bf16[4,2,256,3,64]{2,1,0,4,3:T(2,128)(2,1)}, bf16[4,2,256,3,64]{2,1,0,4,3:T(2,128)(2,1...) while((s32[]{:T(128)}, ...), condition=%wide.region_18.19_spmd, body=%wide.region_16.18_spmd.sunk | while | flops 257789440 | bytes 21261944 | solution.py:295
  367.6 2.7 subtract_exponential_fusion.2
  371.4 2.5 fusion.186
  373.9 3.5 fusion.189
  380.4 3.5 fusion.187
  384.9 2.7 subtract_exponential_fusion.2
  388.7 2.5 fusion.186
  391.2 3.5 fusion.189
  397.7 3.5 fusion.187
  402.2 2.7 subtract_exponential_fusion.2
  406.0 2.5 fusion.186
  408.5 3.5 fusion.189
  415.0 3.4 fusion.187
  419.6 2.7 subtract_exponential_fusion.2
  423.3 2.5 fusion.186
  425.8 3.5 fusion.189
  432.3 3.4 fusion.187
  436.6 3.2 reshape.263
  439.8 3.1 reshape.262
  442.9 3.3 reshape.261
  446.3 2.3 fusion.83
  449.7 2.8 add_convert_fusion
  452.7 7.1 convolution_bitcast_fusion
  459.7 4.1 convolution_bitcast_fusion.1
  473.2 17.5 %reduce-scatter.11.cloned.1.call-done = bf16[512,768]{1,0:T(8,128)(2,1)} async-done(((bf16[2048,768]{1,0:T(8,128)(2,1)}), bf16[512,768]{1,0:T(8,128)(2,1)}) %reduce-scatter.11.cloned.1.call-update) | async-done | bytes 786448 | tf_op jit(solution)/shard_map/reduce_scatter | solution.py:315
  492.6 2.0 fusion.70
  500.6 3.1 fusion.101
  505.8 23.1 %psum.139 = f32[1,768]{1,0:T(1,128)} all-reduce(f32[1,768]{1,0:T(1,128)S(1)} %stack.33), channel_id=1, replica_groups=mesh['rows'=8,'heads'=4] {'rows'}, use_global_device_ids=true, to_apply=%region_48.49 | all-reduce | flops 768 | bytes 6144 | tf_op jit(solution)/shard_map/psum | solution.py:368
  529.0 41.2 %all-reduce.6 = (f32[768]{0:T(1024)}, f32[1,768]{1,0:T(1,128)}, f32[1,768]{1,0:T(1,128)}, f32[1,768]{1,0:T(1,128)}, f32[1,768]{1,0:T(1,128)}, /*index=5*/f32[1,768]{1,0:T(1,128)}, f32[96]{0:T(128)}) all-reduce(f32[768]{0:T(1024)S(1)} %get-tuple-element.235, ...), channel_id=1, replica_groups=mesh['rows'=8,'heads'=4] {'rows','heads'}, use_global_device_ids=true, to_apply=%region_27.28 | all-reduce | flops 4704 | bytes 37632 | tf_op jit(solution)/shard_map/psum | solution.py:383
  571.1 164.5 %all-reduce.14.cloned.1.call-done = (f32[1,768,192]{1,2,0:T(8,128)}, f32[1,768,192]{1,2,0:T(8,128)}, f32[1,768,192]{1,2,0:T(8,128)}, f32[1,192,768]{2,1,0:T(8,12...) async-done(((f32[1,768,192]{1,2,0:T(8,128)}, f32[1,768,192]{1,2,0:T(8,128)}, f32[1,768,192]{1,2,0:T(8,128)}, f32[1,192,768]{2,1,0:T(8,128)}, f32[1,768,768]{2,1,0:T(8,128)}, ...) | async-done | bytes 7077904 | tf_op jit(solution)/shard_map/psum | solution.py:368
  735.6 152.2 %all-reduce.12.cloned.1.call-done = (f32[48,768]{1,0:T(8,128)}, f32[256,768]{1,0:T(8,128)}, f32[1000,768]{1,0:T(8,128)}, f32[768,96]{0,1:T(8,128)}) async-done(((f32[48,768]{1,0:T(8,128)}, f32[256,768]{1,0:T(8,128)}, f32[1000,768]{1,0:T(8,128)}, f32[768,96]{0,1:T(8,128)}), (f32[48,768]{1,0:T(8,128)}, f32[256,768]{1,0:T(8,128)}, f32[1000,768]{1,0:T(8,128)}, ...) | async-done | bytes 4300816 | tf_op jit(solution)/shard_map/psum | solution.py:383
  889.4 2.1 copy.166
  891.5 3.8 copy.167
  (307 shorter events, 99.0 us)
Async XLA Ops:
  7.2 4.8 copy-start
  7.2 4.8 copy-start.59
  7.2 39.1 %all-gather.4.cloned.1.call-start = ((), (), s32[]{:S(2)}) async-start(), calls=%async_computation.4 | async-start | bytes 3932160 | tf_op jit(solution)/shard_map/all_gather | solution.py:158
  12.0 1.6 copy-start.47
  12.0 1.6 copy-start.48
  13.3 1.8 copy-start.43
  13.3 33.0 %copy-start.39 = (bf16[1,768,192]{1,2,0:T(8,128)(2,1)S(1)}, bf16[1,768,192]{1,2,0:T(8,128)(2,1)}, u32[]{:S(2)}) copy-start(bf16[1,768,192]{1,2,0:T(8,128)(2,1)} %param.38) | copy-start | bytes 884740
  14.9 114.4 %reduce-scatter.5.cloned.1.call-start = ((), (), s32[]{:S(2)}) async-start(), calls=%async_computation.5 | async-start | bytes 3932160 | tf_op jit(solution)/shard_map/reduce_scatter | solution.py:167
  49.3 2.8 copy-start.33
  56.1 5.5 copy-start.31
  72.2 16.2 %copy-start.37 = (bf16[1,192,768]{2,1,0:T(8,128)(2,1)S(1)}, bf16[1,192,768]{2,1,0:T(8,128)(2,1)}, u32[]{:S(2)}) copy-start(bf16[1,192,768]{2,1,0:T(8,128)(2,1)} %param.39) | copy-start | bytes 884740
  91.2 70.6 %all-gather.6.cloned.1.call-start = ((), (), s32[]{:S(2)}) async-start(), calls=%async_computation.6 | async-start | bytes 3932160 | tf_op jit(solution)/shard_map/all_gather | solution.py:172
  130.7 2.6 copy-start.46
  133.1 91.3 %reduce-scatter.7.cloned.1.call-start = ((), (), s32[]{:S(2)}) async-start(), calls=%async_computation.7 | async-start | bytes 3932160 | tf_op jit(solution)/shard_map/reduce_scatter | solution.py:178
  161.7 20.5 %copy-start.56 = (bf16[1,768,768]{2,1,0:T(8,128)(2,1)S(1)}, bf16[1,768,768]{2,1,0:T(8,128)(2,1)}, u32[]{:S(2)}) copy-start(bf16[1,768,768]{2,1,0:T(8,128)(2,1)} %param.44) | copy-start | bytes 3538948
  180.6 1.7 copy-start.60
  186.2 40.8 %copy-start.24 = (bf16[768,96]{0,1:T(8,128)(2,1)S(1)}, bf16[768,96]{0,1:T(8,128)(2,1)}, u32[]{:S(2)}) copy-start(bf16[768,96]{0,1:T(8,128)(2,1)} %param.46) | copy-start | bytes 442372
  186.2 41.1 %copy-start.54 = (f32[96]{0:T(128)S(1)}, f32[96]{0:T(128)}, u32[]{:S(2)}) copy-start(f32[96]{0:T(128)} %param.47) | copy-start | bytes 1156
  186.2 133.9 %reduce-scatter.9.cloned.1.call-start = ((), (), s32[]{:S(2)}) async-start(), calls=%async_computation.8 | async-start | bytes 3932160 | tf_op jit(solution)/shard_map/reduce_scatter | solution.py:281
  187.2 40.4 %copy-start.23 = (f32[512,48]{0,1:T(8,128)S(1)}, f32[512,48]{0,1:T(8,128)}, u32[]{:S(2)}) copy-start(f32[512,48]{0,1:T(8,128)} %param.27) | copy-start | bytes 294916
  187.2 40.5 %copy-start.29 = (f32[512,48]{0,1:T(8,128)S(1)}, f32[512,48]{0,1:T(8,128)}, u32[]{:S(2)}) copy-start(f32[512,48]{0,1:T(8,128)} %param.48) | copy-start | bytes 294916
  232.9 19.6 %collective-permute-start = (bf16[512,768]{1,0:T(8,128)(2,1)}, bf16[512,768]{1,0:T(8,128)(2,1)}, u32[]{:S(2)}, u32[]{:S(2)}) collective-permute-start(bf16[512,768]{1,0:T(8,128)(2,1)} %get-tuple-element.240), channel_id=1, source_target_pairs={{0,1},{1,2},{2,3},{3,0},{4,5},{5,6},{6,7},{7,4},{8,9},{9,10},{10,1... | collective-permute-start | bytes 2359304 | tf_op jit(solution)/shard_map/ppermute | solution.py:265
  232.9 21.8 %collective-permute-start.1 = (bf16[512,768]{1,0:T(8,128)(2,1)}, bf16[512,768]{1,0:T(8,128)(2,1)}, u32[]{:S(2)}, u32[]{:S(2)}) collective-permute-start(bf16[512,768]{1,0:T(8,128)(2,1)} %get-tuple-element.240), channel_id=1, source_target_pairs={{0,3},{1,0},{2,1},{3,2},{4,7},{5,4},{6,5},{7,6},{8,11},{9,8},{10,9... | collective-permute-start | bytes 2359304 | tf_op jit(solution)/shard_map/ppermute | solution.py:270
  252.5 11.7 %collective-permute-start.2 = (bf16[512,768]{1,0:T(8,128)(2,1)}, bf16[512,768]{1,0:T(8,128)(2,1)}, u32[]{:S(2)}, u32[]{:S(2)}) collective-permute-start(bf16[512,768]{1,0:T(8,128)(2,1)} %collective-permute-done), channel_id=1, source_target_pairs={{0,1},{1,2},{2,3},{3,0},{4,5},{5,6},{6,7},{7,4},{8,9},{9,10},{10,1... | collective-permute-start | bytes 2359304 | tf_op jit(solution)/shard_map/ppermute | solution.py:265
  252.5 13.8 %copy-start.57 = (bf16[1,768,768]{2,1,0:T(8,128)(2,1)S(1)}, bf16[1,768,768]{2,1,0:T(8,128)(2,1)}, u32[]{:S(2)}) copy-start(bf16[1,768,768]{2,1,0:T(8,128)(2,1)} %param.44) | copy-start | bytes 3538948
  266.3 11.8 %copy-start.58 = (bf16[1,768,768]{2,1,0:T(8,128)(2,1)S(1)}, bf16[1,768,768]{2,1,0:T(8,128)(2,1)}, u32[]{:S(2)}) copy-start(bf16[1,768,768]{2,1,0:T(8,128)(2,1)} %param.42) | copy-start | bytes 3538948
  276.5 1.7 copy-start.61
  282.2 74.1 %all-gather.8.cloned.1.call-start = ((), (), s32[]{:S(2)}) async-start(), calls=%async_computation.9 | async-start | bytes 3932160 | tf_op jit(solution)/shard_map/all_gather | solution.py:291
  320.1 3.0 copy-start.20
  323.1 3.4 copy-start.6
  325.2 1.2 copy-start.8
  326.5 29.8 %copy-start.38 = (bf16[1,192,768]{2,1,0:T(8,128)(2,1)S(1)}, bf16[1,192,768]{2,1,0:T(8,128)(2,1)}, u32[]{:S(2)}) copy-start(bf16[1,192,768]{2,1,0:T(8,128)(2,1)} %param.39) | copy-start | bytes 884740
  327.6 163.1 %reduce-scatter.11.cloned.1.call-start = ((), (), s32[]{:S(2)}) async-start(), calls=%async_computation.10 | async-start | bytes 3932160 | tf_op jit(solution)/shard_map/reduce_scatter | solution.py:315
  436.6 9.6 %copy-start.32 = (bf16[1,768,192]{1,2,0:T(8,128)(2,1)S(1)}, bf16[1,768,192]{1,2,0:T(8,128)(2,1)}, u32[]{:S(2)}) copy-start(bf16[1,768,192]{1,2,0:T(8,128)(2,1)} %param.37) | copy-start | bytes 884740
  446.2 2.3 copy-start.12
  446.2 2.3 copy-start.34
  448.5 1.2 copy-start.40
  452.6 283.1 %all-reduce.14.cloned.1.call-start = ((), (), s32[]{:S(2)}) async-start(), calls=%async_computation.12 | async-start | bytes 14155776 | tf_op jit(solution)/shard_map/psum | solution.py:368
  452.6 7.1 copy-start.55
  452.6 7.1 copy-start.62
  459.7 4.1 copy-start.19
  463.9 2.1 copy-start.5
  463.9 2.3 copy-start.15
  466.2 1.6 copy-start.11
  467.8 1.6 copy-start.13
  471.0 1.2 copy-start.17
  471.1 416.8 %all-reduce.12.cloned.1.call-start = ((), (), s32[]{:S(2)}) async-start(), calls=%async_computation.11 | async-start | bytes 8601600 | tf_op jit(solution)/shard_map/psum | solution.py:383
  490.7 3.9 copy-start.7
  490.7 3.9 copy-start.9
  490.7 3.9 copy-start.18
  496.7 1.9 copy-start.4
  503.8 2.1 copy-start.45
  503.8 25.2 %copy-start.42 = (f32[768]{0:T(1024)S(1)}, f32[768]{0:T(1024)}, u32[]{:S(2)}) copy-start(f32[768]{0:T(1024)} %get-tuple-element.173) | copy-start | bytes 9220
  503.8 25.2 %copy-start.41 = (f32[768]{0:T(1024)S(1)}, f32[768]{0:T(1024)}, u32[]{:S(2)}) copy-start(f32[768]{0:T(1024)} %get-tuple-element.177) | copy-start | bytes 9220
  503.8 66.4 %copy-start.30 = (f32[512,48]{0,1:T(8,128)S(1)}, f32[512,48]{0,1:T(8,128)}, u32[]{:S(2)}) copy-start(f32[512,48]{0,1:T(8,128)} %param.48) | copy-start | bytes 294916
  503.8 66.4 %copy-start.36 = (bf16[48,768]{1,0:T(8,128)(2,1)S(1)}, bf16[48,768]{1,0:T(8,128)(2,1)}, u32[]{:S(2)}) copy-start(bf16[48,768]{1,0:T(8,128)(2,1)} %param.30) | copy-start | bytes 221188
  891.5 3.8 copy-start.28
  891.5 4.7 copy-start.27
  891.5 5.5 copy-start.26
  895.3 2.5 copy-start.25
  895.3 3.3 copy-start.22
  898.6 2.5 copy-start.21
  898.6 4.6 copy-start.1
  901.1 1.4 copy-start.35
  (11 other events, 9.5 us)
Sparse Core Ops, SparseCore 0:
  15.0 31.2 all-gather.3
  91.3 37.9 reduce-scatter.4
  133.2 28.5 all-gather.5
  186.3 37.9 reduce-scatter.6
  282.3 37.7 reduce-scatter.8
  327.7 28.5 all-gather.7
  452.7 37.9 reduce-scatter.10
  496.9 238.6 all-reduce.13
  744.6 143.1 all-reduce.11
